TPU v7x, 128 devices: a whole 4x4x4 slice. The times are simulated.
128 devices in a mesh: expert: 8 (over y_lo, x), tile: 16 (over z, y_hi, core).
Axes of the slice: x: 4, y: 4 (y_hi: 2, y_lo: 2; y = y_hi * 2 + y_lo), z: 4, core: 2. Of those that a mesh axis runs over, the one named last changes fastest.
Arguments:
- activations: bfloat16 [6144, 6144], P(('expert', 'tile')), may hold values from -40 to 40
- expert_ids: int32 [6144, 2], P(('expert', 'tile')), may hold values from 0 to 7, all different within a row; in each aligned block of 48 rows (0 to 47, 48 to 95, ...) at most 24 rows name the same one
Outputs:
- hessian: float32 [8, 6144, 6144], P('expert', 'tile')
- panels: float32 [8, 6144, 1536], P('expert', 'tile')
Inputs may be any that keep to these rules, and one draw needn't show every extreme that they name: `expert_ids`: each row names 2 different experts; within the rows of one device no expert is named more than 24 times, a bound that some block reaches; every expert is named by some row.
All inputs are finite; a program needn't handle non-finite values.
Results may differ from a plain program's by a relative error of at most 0.0003.
Values may be sent and summed in bfloat16 or wider, within the bound.
No kernel may reach another device: no remote copies, remote signals or barrier semaphores. Data moves between devices by JAX's collectives and lax.ppermute only.
A program may use at most 256 MiB of HBM per device.

v0:
```python
import math

import jax
import jax.numpy as jnp
from jax import lax
from jax.sharding import PartitionSpec as P

PANEL = 768


damp_fraction = 0.01


def side_by_side(arrays, axis, split_dim, concat_dim, along):
    widths = [math.prod(a.shape[along:]) for a in arrays]
    both = jnp.concatenate(
        [a.reshape(*a.shape[:along], w) for a, w in zip(arrays, widths)], axis=along
    )
    out = lax.all_to_all(both, axis, split_axis=split_dim, concat_axis=concat_dim, tiled=True)
    blocks = jnp.split(out, [sum(widths[:k]) for k in range(1, len(widths))], axis=along)
    return tuple((b.reshape(*out.shape[:along], *a.shape[along:]) for a, b in zip(arrays, blocks)))


def copy_for_each(x, axis):
    count = lax.axis_size(axis)
    return lax.all_to_all(jnp.broadcast_to(x[None], (count, *x.shape)), axis, 0, 0, tiled=True)


def taken_together(x, axis):
    return copy_for_each(x, axis).sum(axis=0)


def local(activations, expert_ids):
    tile_count = lax.axis_size("tile")
    group_count = lax.axis_size("expert")
    token_count = activations.shape[0]
    feature_width = activations.shape[1]
    capacity = 2 * token_count * expert_ids.shape[1] // group_count
    rows_device = feature_width // tile_count
    tile_index = lax.axis_index("tile")
    expert_iota = jnp.arange(group_count, dtype=jnp.int32)
    global_rows = tile_index * rows_device + jnp.arange(rows_device, dtype=jnp.int32)
    routed = jnp.sum((expert_ids[None][..., None] == expert_iota).astype(jnp.int32), axis=2)
    slot_index = jnp.cumsum(routed, axis=1) - 1
    slot_iota = jnp.arange(capacity, dtype=jnp.int32)
    selector = (routed[..., None] > 0) & (slot_index[..., None] == slot_iota)
    packed = jnp.einsum(
        "nkes,nkd->ensd",
        selector.astype(jnp.bfloat16),
        activations[None],
        preferred_element_type=jnp.float32,
    ).astype(jnp.bfloat16)
    flags = jnp.transpose(jnp.sum(selector.astype(jnp.float32), axis=1), (1, 0, 2)).astype(
        jnp.bfloat16
    )
    send_rows = packed
    send_flags = flags
    send_rows = send_rows.reshape(group_count, capacity, feature_width)
    send_flags = send_flags.reshape(group_count, capacity)
    received_rows, received_flags = side_by_side((send_rows, send_flags), "expert", 0, 0, 2)
    accumulate_received_rows = lax.all_gather(
        received_rows.reshape(group_count * capacity, feature_width), "tile", axis=0, tiled=True
    )
    accumulate_received_flags = lax.all_gather(
        received_flags.reshape(group_count * capacity), "tile", axis=0, tiled=True
    )
    own_columns = lax.dynamic_slice_in_dim(
        accumulate_received_rows, tile_index * rows_device, rows_device, 1
    )
    total = jnp.einsum(
        "tr,tc->rc", own_columns, accumulate_received_rows, preferred_element_type=jnp.float32
    )
    expert_count = jnp.sum(accumulate_received_flags.astype(jnp.float32))
    hessian = total * (2.0 / expert_count)
    diag_mask = global_rows[:, None] == jnp.arange(feature_width, dtype=jnp.int32)[None, :]
    diag_total = taken_together(jnp.sum(jnp.where(diag_mask, hessian, jnp.float32(0.0))), "tile")
    damping = damp_fraction * diag_total / feature_width
    hessian = hessian + jnp.where(diag_mask, damping, jnp.float32(0.0))

    def panel_rows_fetch(members, panel_start):
        placement = (
            panel_start + jnp.arange(PANEL, dtype=jnp.int32)[:, None] == global_rows[None, :]
        ).astype(jnp.float32)
        placed = tuple(
            (
                jnp.dot(placement, member_rows, precision=lax.Precision.HIGHEST)
                for member_rows in members
            )
        )
        return lax.psum(placed, "tile")

    factors = []
    for panel in range(2):
        panel_start = panel * PANEL
        panel_block = hessian[:, panel_start : panel_start + PANEL]
        if factors:
            diagonal_rows, earlier_rows = panel_rows_fetch((panel_block, factors[0]), panel_start)
            panel_block = panel_block - jnp.dot(
                factors[0], earlier_rows.T, precision=lax.Precision.HIGHEST
            )
            diagonal_block = diagonal_rows - jnp.dot(
                earlier_rows, earlier_rows.T, precision=lax.Precision.HIGHEST
            )
        else:
            diagonal_block = panel_rows_fetch((panel_block,), panel_start)[0]
        diagonal_factor = jnp.linalg.cholesky(diagonal_block)
        panel_factor = jax.scipy.linalg.solve_triangular(
            diagonal_factor, panel_block.T, lower=True
        ).T
        column_index = panel_start + jnp.arange(PANEL, dtype=jnp.int32)
        lower_mask = global_rows[:, None] >= column_index[None, :]
        factors.append(jnp.where(lower_mask, panel_factor, jnp.float32(0.0)))
    return (hessian[None], jnp.concatenate(factors, axis=1)[None])


def solution(mesh):
    placed = (P(("expert", "tile"), None), P(("expert", "tile"), None))
    return jax.shard_map(
        local,
        mesh=mesh,
        in_specs=placed,
        out_specs=(P("expert", "tile", None), P("expert", "tile", None)),
        check_vma=False,
    )
```

profile of v0, /device:TPU:0, one launch (start us, length us, event | category | flops | bytes accessed | tf_op | source)
XLA Modules:
  0.0 1108.4 jit_solution(1316372026263907840)
XLA Ops:
  9.4 36.0 %all_to_all.11 = bf16[8,24,6145]{2,1,0:T(8,128)(2,1)S(1)} all-to-all(bf16[8,24,6145]{2,1,0:T(8,128)(2,1)S(1)} %pad_maximum_fusion), channel_id=1, replica_groups=mesh['expert'=8,'tile'=16] {'expert'}, dimensions={0} | all-to-all | bytes 4719360 | tf_op jit(solution)/shard_map/all_to_all | solution.py:19
  49.4 39.8 %all-reduce.1 = bf16[3072]{0:T(1024)(128)(2,1)S(1)} all-reduce(bf16[3072]{0:T(1024)(128)(2,1)S(1)} %dynamic-update-slice.25), channel_id=1, replica_groups=mesh['expert'=8,'tile'=16] {'tile'}, use_global_device_ids=true, to_apply=%add.1 | all-reduce | flops 3072 | bytes 12288
  90.5 162.6 %all-gather.2.cloned.1.call-done = bf16[3072,6144]{1,0:T(8,128)(2,1)} async-done(((bf16[192,6144]{1,0:T(8,128)(2,1)}), bf16[3072,6144]{1,0:T(8,128)(2,1)}) %all-gather.2.cloned.1.call-update) | async-done | bytes 37748752 | tf_op jit(solution)/shard_map/all_gather | solution.py:61
  253.1 24.2 %select_reduce_fusion = (f32[]{:T(128)}, f32[384,6144]{1,0:T(8,128)}) fusion(s32[384]{0:T(512)S(1)} %iota_add_fusion.1, f32[]{:T(128)S(6)} %div.12, bf16[3072,6144]{1,0:T(8,128)(2,1)} %all-gather.2.cloned.1.call-done, s32[]{:T(128)S(6)} %select_n.21), kind=kOutput, calls=%fused_computation.5 | convolution fusion | flops 14504951808 | bytes 49546764 | tf_op jit(solution)/shard_map/tr,tc->rc/dot_general | solution.py:70
  310.4 137.7 %all-reduce.6.cloned.1.call-done = f32[768,768]{0,1:T(8,128)} async-done(((f32[768,768]{0,1:T(8,128)}), f32[768,768]{0,1:T(8,128)}) %all-reduce.6.cloned.1.call-update) | async-done | bytes 2359312 | tf_op jit(solution)/shard_map/psum | solution.py:90
  454.7 11.7 %cholesky.453 = f32[128,128]{1,0:T(8,128)S(1)} custom-call(f32[128,128]{1,0:T(8,128)S(1)} %cholesky.669), custom_call_target="Cholesky" | custom-call | tf_op jit(solution)/shard_map/jit(cholesky)/cholesky | solution.py:106
  479.2 11.7 %cholesky.472 = f32[128,128]{1,0:T(8,128)S(1)} custom-call(f32[128,128]{1,0:T(8,128)S(1)} %cholesky.673), custom_call_target="Cholesky" | custom-call | tf_op jit(solution)/shard_map/jit(cholesky)/cholesky | solution.py:106
  491.0 10.2 custom-call.42
  503.1 11.7 %cholesky.493 = f32[128,128]{1,0:T(8,128)S(1)} custom-call(f32[128,128]{1,0:T(8,128)S(1)} %cholesky.678), custom_call_target="Cholesky" | custom-call | tf_op jit(solution)/shard_map/jit(cholesky)/cholesky | solution.py:106
  527.3 11.9 %cholesky.512 = f32[128,128]{1,0:T(8,128)S(1)} custom-call(f32[128,128]{1,0:T(8,128)S(1)} %cholesky.683), custom_call_target="Cholesky" | custom-call | tf_op jit(solution)/shard_map/jit(cholesky)/cholesky | solution.py:106
  551.4 11.7 %cholesky.531 = f32[128,128]{1,0:T(8,128)S(1)} custom-call(f32[128,128]{1,0:T(8,128)S(1)} %cholesky.688), custom_call_target="Cholesky" | custom-call | tf_op jit(solution)/shard_map/jit(cholesky)/cholesky | solution.py:106
  575.2 12.1 %cholesky.548 = f32[128,128]{1,0:T(8,128)S(1)} custom-call(f32[128,128]{1,0:T(8,128)S(1)} %convolution_subtract_fusion.21), custom_call_target="Cholesky" | custom-call | tf_op jit(solution)/shard_map/jit(cholesky)/cholesky | solution.py:106
  594.0 17.5 %while.4 = (s32[]{:T(128)}, f32[768,768]{1,0:T(8,128)}, s32[6,2]{0,1:T(2,128)S(1)}, f32[6,128,128]{2,1,0:T(8,128)S(1)}, s32[]{:T(128)}) while((s32[]{:T(128)}, f32[768,768]{1,0:T(8,128)}, s32[6,2]{0,1:T(2,128)S(1)}, f32[6,128,128]{2,1,0:T(8,128)S(1)}, s32[]{:T(128)}) %tuple.86), condition=%wide.while_cond, body=%wide.while_body.sunk | while | flops 2 | bytes 131181 | solution.py:107
  611.5 59.0 %custom-call.46 = f32[6,128,128]{1,2,0:T(8,128)S(1)} custom-call(f32[6,128,128]{2,1,0:T(8,128)S(1)} %get-tuple-element.18), custom_call_target="InvertDiagBlocksLowerTriangular" | custom-call | tf_op jit(solution)/shard_map/jit(_solve_triangular)/triangular_solve | solution.py:107
  697.3 151.3 %all-reduce.8.cloned.1.call-done = (f32[768,768]{1,0:T(8,128)}, f32[768,768]{0,1:T(8,128)}) async-done(((f32[768,768]{1,0:T(8,128)}, f32[768,768]{0,1:T(8,128)}), (f32[768,768]{1,0:T(8,128)}, f32[768,768]{0,1:T(8,128)})) %all-reduce.8.cloned.1.call-update) | async-done | bytes 4718608 | tf_op jit(solution)/shard_map/psum | solution.py:90
  869.1 11.7 %cholesky.563 = f32[128,128]{1,0:T(8,128)S(1)} custom-call(f32[128,128]{1,0:T(8,128)S(1)} %cholesky.692), custom_call_target="Cholesky" | custom-call | tf_op jit(solution)/shard_map/jit(cholesky)/cholesky | solution.py:106
  893.6 11.7 %cholesky.582 = f32[128,128]{1,0:T(8,128)S(1)} custom-call(f32[128,128]{1,0:T(8,128)S(1)} %cholesky.696), custom_call_target="Cholesky" | custom-call | tf_op jit(solution)/shard_map/jit(cholesky)/cholesky | solution.py:106
  906.7 10.2 custom-call.48
  918.8 11.7 %cholesky.603 = f32[128,128]{1,0:T(8,128)S(1)} custom-call(f32[128,128]{1,0:T(8,128)S(1)} %cholesky.701), custom_call_target="Cholesky" | custom-call | tf_op jit(solution)/shard_map/jit(cholesky)/cholesky | solution.py:106
  942.9 11.8 %cholesky.622 = f32[128,128]{1,0:T(8,128)S(1)} custom-call(f32[128,128]{1,0:T(8,128)S(1)} %cholesky.706), custom_call_target="Cholesky" | custom-call | tf_op jit(solution)/shard_map/jit(cholesky)/cholesky | solution.py:106
  967.0 11.7 %cholesky.641 = f32[128,128]{1,0:T(8,128)S(1)} custom-call(f32[128,128]{1,0:T(8,128)S(1)} %cholesky.711), custom_call_target="Cholesky" | custom-call | tf_op jit(solution)/shard_map/jit(cholesky)/cholesky | solution.py:106
  990.7 11.9 %cholesky.658 = f32[128,128]{1,0:T(8,128)S(1)} custom-call(f32[128,128]{1,0:T(8,128)S(1)} %convolution_subtract_fusion.20), custom_call_target="Cholesky" | custom-call | tf_op jit(solution)/shard_map/jit(cholesky)/cholesky | solution.py:106
  1008.6 17.9 %while.5 = (s32[]{:T(128)}, f32[768,768]{1,0:T(8,128)}, s32[6,2]{0,1:T(2,128)S(1)}, f32[6,128,128]{2,1,0:T(8,128)S(1)}, s32[]{:T(128)}) while((s32[]{:T(128)}, f32[768,768]{1,0:T(8,128)}, s32[6,2]{0,1:T(2,128)S(1)}, f32[6,128,128]{2,1,0:T(8,128)S(1)}, s32[]{:T(128)}) %tuple.99), condition=%wide.while_cond.clone, body=%wide.while_body.clone.sunk | while | flops 2 | bytes 131181 | solution.py:107
  1026.5 59.0 %custom-call.52 = f32[6,128,128]{1,2,0:T(8,128)S(1)} custom-call(f32[6,128,128]{2,1,0:T(8,128)S(1)} %get-tuple-element.19), custom_call_target="InvertDiagBlocksLowerTriangular" | custom-call | tf_op jit(solution)/shard_map/jit(_solve_triangular)/triangular_solve | solution.py:107
  (198 shorter events, 252.8 us)
Async XLA Ops:
  7.2 1.2 copy-start
  7.2 245.9 %all-gather.2.cloned.1.call-start = ((), (), s32[]{:S(2)}) async-start(), calls=%async_computation.2 | async-start | bytes 40108032 | tf_op jit(solution)/shard_map/all_gather | solution.py:61
  47.1 0.7 copy-start.12
  278.5 10.9 all-to-all-start.1
  282.0 166.1 %all-reduce.6.cloned.1.call-start = ((), (), s32[]{:S(2)}) async-start(), calls=%async_computation.3 | async-start | bytes 4718592 | tf_op jit(solution)/shard_map/psum | solution.py:90
  295.6 3.6 copy-start.2
  302.8 545.8 %all-reduce.8.cloned.1.call-start = ((), (), s32[]{:S(2)}) async-start(), calls=%async_computation.4 | async-start | bytes 9437184 | tf_op jit(solution)/shard_map/psum | solution.py:90
  448.1 3.2 copy-start.6
  453.3 1.4 copy-start.8
  593.9 79.7 %copy-start.9 = (f32[768,384]{0,1:T(8,128)S(1)}, f32[768,384]{0,1:T(8,128)}, u32[]{:S(2)}) copy-start(f32[768,384]{0,1:T(8,128)} %slice_bitcast_fusion) | copy-start | bytes 3538948
  684.3 164.3 %copy-start.4 = (f32[384,768]{0,1:T(8,128)}, f32[384,768]{0,1:T(8,128)S(1)}, u32[]{:S(2)}) copy-start(f32[384,768]{0,1:T(8,128)S(1)} %bitcast_select_fusion.1) | copy-start | bytes 3538948
  848.6 9.0 copy-start.3
  848.6 9.0 copy-start.11
  867.7 1.4 copy-start.7
  1008.6 80.1 %copy-start.10 = (f32[768,384]{0,1:T(8,128)S(1)}, f32[768,384]{0,1:T(8,128)}, u32[]{:S(2)}) copy-start(f32[768,384]{0,1:T(8,128)} %fusion.7) | copy-start | bytes 3538948
  1096.1 3.4 copy-start.5
  1099.5 2.1 copy-start.1
Sparse Core Ops, SparseCore 0:
  47.2 205.8 all-gather.1
  302.9 145.1 all-reduce.5
  687.9 160.5 all-reduce.7
where the time goes:
time: 1120 us; the launch traced here: 1110 us
  waiting for transfers between devices  459 us (41%)
  other arithmetic  390 us (35%)
  matrix products  98.9 us (9%)
  blocking collectives  75.8 us (7%)
  local copies, waits for them, and re-layouts  56.5 us (5%)
  between operations  24.1 us (2%)
    psum x2, waiting for transfers between devices, panel_rows_fetch(): return lax.psum(placed, 'tile')  289 us
    another operation x45, other arithmetic, local(): diagonal_factor = jnp.linalg.cholesky(diagonal_block)  248 us
    all_gather x1, waiting for transfers between devices, local(): lax.all_gather(received_rows.reshape(group_count * capacity, feature_widt...  163 us
    another operation x5, other arithmetic, local(): jax.scipy.linalg.solve_triangular(diagonal_factor, panel_block.T, lower=T...  121 us
    unnamed x1, blocking collectives  39.8 us
    all_to_all x1, blocking collectives, side_by_side(): lax.all_to_all(both, axis, split_axis=split_dim, concat_axis=concat_dim,...  36 us
    another operation x39, local copies, waits for them, and re-layouts, local(): jax.scipy.linalg.solve_triangular(diagonal_factor, panel_block.T, lower=T...  35.3 us
    another operation x22, matrix products, local(): jax.scipy.linalg.solve_triangular(diagonal_factor, panel_block.T, lower=T...  27.3 us
  transfers between devices with their start and end apart: 4, of which 4 were waited for; matrix products, arithmetic and copies ran while one was open for 2% of the time, Pallas kernels for 0%

commit v1 on v0

v1 whole, which is shorter than its diff:
```python
import jax
import jax.numpy as jnp
from jax import lax
from jax.experimental import pallas as pl
from jax.experimental.pallas import tpu as pltpu
from jax.sharding import PartitionSpec as P

PANEL = 768
LEAD = 2 * PANEL
EXTRA = 128
BLOCK = 256
HALF = 128
MICRO = 8
DAMP = 0.01

f32 = jnp.float32
bf16 = jnp.bfloat16


def lane_fill(column):
    return jnp.broadcast_to(column, (column.shape[0], HALF))


def row_fill(block, i):
    return jnp.broadcast_to(block[i : i + 1, :], block.shape)


def tree_sum(terms):
    terms = list(terms)
    while len(terms) > 1:
        terms = [
            terms[i] + terms[i + 1] if i + 1 < len(terms) else terms[i]
            for i in range(0, len(terms), 2)
        ]
    return terms[0]


def inverse_factor(read, write):
    groups = HALF // MICRO
    sub = lax.broadcasted_iota(jnp.int32, (MICRO, HALF), 0)
    lane = lax.broadcasted_iota(jnp.int32, (MICRO, HALF), 1)
    a = [read(g) for g in range(groups)]
    e = [(lane == sub + MICRO * g).astype(f32) for g in range(groups)]
    for g in range(groups):
        first = MICRO * g
        cols = [lane_fill(a[g][:, first + c : first + c + 1]) for c in range(MICRO)]
        forward, full_a, full_e = e[g], a[g], e[g]
        pivots = None
        for i in range(MICRO):
            r = 1.0 / row_fill(cols[i], i)
            pivots = r if pivots is None else jnp.where(sub >= i, r, pivots)
            scaled = cols[i] * r
            both = jnp.where(sub == i, 1.0 - r, scaled)
            below = jnp.where(sub > i, scaled, 0.0)
            for c in range(i + 1, MICRO):
                cols[c] = cols[c] - both * row_fill(cols[c], i)
            forward = forward - below * row_fill(forward, i)
            full_a = full_a - both * row_fill(full_a, i)
            full_e = full_e - both * row_fill(full_e, i)
        write(g, forward * jnp.sqrt(pivots))
        if g + 1 == groups:
            break
        rows_a = [row_fill(full_a, i) for i in range(MICRO)]
        rows_e = [row_fill(full_e, i) for i in range(MICRO)]
        for q in range(g + 1, groups):
            coef = [lane_fill(a[q][:, first + i : first + i + 1]) for i in range(MICRO)]
            a[q] = a[q] - tree_sum([coef[i] * rows_a[i] for i in range(MICRO)])
            e[q] = e[q] - tree_sum([coef[i] * rows_e[i] for i in range(MICRO)])


def split(x):
    hi = x.astype(bf16)
    return hi, (x - hi.astype(f32)).astype(bf16)


def dot_t(a, b):
    return lax.dot_general(a, b, (((1,), (1,)), ((), ())), preferred_element_type=f32)


def dot3(a, b):
    return dot_t(a[0], b[0]) + (dot_t(a[0], b[1]) + dot_t(a[1], b[0]))


def exact_t(a, b):
    return lax.dot_general(
        a, b, (((1,), (1,)), ((), ())), precision=lax.Precision.HIGHEST, preferred_element_type=f32
    )


def exact(a, b):
    return jnp.dot(a, b, precision=lax.Precision.HIGHEST, preferred_element_type=f32)


def blk(i):
    return pl.ds(pl.multiple_of(i * BLOCK, BLOCK), BLOCK)


def cholesky_kernel(scalars, gram, lh, lm, wh, wm, col, dd, wd, lower):
    count = LEAD // BLOCK
    scale = scalars[0]
    damping = scalars[1]
    eye = (
        lax.broadcasted_iota(jnp.int32, (BLOCK, BLOCK), 0)
        == lax.broadcasted_iota(jnp.int32, (BLOCK, BLOCK), 1)
    ).astype(f32)

    @pl.loop(0, count)
    def _(j):
        @pl.loop(j, count)
        def _(i):
            col[blk(i), :] = gram[blk(i), blk(j)] * scale

            @pl.loop(0, j)
            def _(k):
                col[blk(i), :] -= dot3(
                    (lh[blk(i), blk(k)], lm[blk(i), blk(k)]),
                    (lh[blk(j), blk(k)], lm[blk(j), blk(k)]),
                )

        diag = col[blk(j), :] + damping * eye
        dd[0] = diag[:HALF, :HALF]
        dd[1] = diag[HALF:, HALF:]
        lower[...] = diag[HALF:, :HALF]

        @pl.loop(0, 2)
        def _(s):
            def write(g, value):
                wd[s, g * MICRO : (g + 1) * MICRO, :] = value

            inverse_factor(lambda g: dd[s, g * MICRO : (g + 1) * MICRO, :], write)

            @pl.when(s == 0)
            def _():
                lower[...] = exact_t(lower[...], wd[0])
                dd[1] = dd[1] - exact_t(lower[...], lower[...])

        corner = -exact(wd[1], exact(lower[...], wd[0]))
        for piece, value in (
            ((slice(0, HALF), slice(0, HALF)), wd[0]),
            ((slice(HALF, BLOCK), slice(0, HALF)), corner),
            ((slice(HALF, BLOCK), slice(HALF, BLOCK)), wd[1]),
            ((slice(0, HALF), slice(HALF, BLOCK)), jnp.zeros((HALF, HALF), f32)),
        ):
            hi, mid = split(value)
            wh[(j, *piece)] = hi
            wm[(j, *piece)] = mid

        @pl.loop(j + 1, count)
        def _(i):
            hi, mid = split(dot3(split(col[blk(i), :]), (wh[j], wm[j])))
            lh[blk(i), blk(j)] = hi
            lm[blk(i), blk(j)] = mid


def cholesky_lead(gram, scalars):
    count = LEAD // BLOCK
    vmem = pl.BlockSpec(memory_space=pltpu.VMEM)
    return pl.pallas_call(
        cholesky_kernel,
        out_shape=(
            jax.ShapeDtypeStruct((LEAD, LEAD), bf16),
            jax.ShapeDtypeStruct((LEAD, LEAD), bf16),
            jax.ShapeDtypeStruct((count, BLOCK, BLOCK), bf16),
            jax.ShapeDtypeStruct((count, BLOCK, BLOCK), bf16),
        ),
        in_specs=[pl.BlockSpec(memory_space=pltpu.SMEM), vmem],
        out_specs=(vmem,) * 4,
        scratch_shapes=[
            pltpu.VMEM((LEAD, BLOCK), f32),
            pltpu.VMEM((2, HALF, HALF), f32),
            pltpu.VMEM((2, HALF, HALF), f32),
            pltpu.VMEM((HALF, HALF), f32),
        ],
        compiler_params=pltpu.CompilerParams(vmem_limit_bytes=40 << 20),
        cost_estimate=pl.CostEstimate(
            flops=150_000_000_000, bytes_accessed=30_000_000, transcendentals=0
        ),
        name="cholesky_lead",
    )(scalars, gram)


def solve_kernel(first_row, rows, lh, lm, wh, wm, out, fh, fm):
    count = LEAD // BLOCK
    rows_device = rows.shape[0]
    row = first_row[0] + lax.broadcasted_iota(jnp.int32, (rows_device, BLOCK), 0)
    lane = lax.broadcasted_iota(jnp.int32, (rows_device, BLOCK), 1)
    for j in range(count):
        here = slice(j * BLOCK, (j + 1) * BLOCK)
        value = rows[:, here]
        for k in range(j):
            there = slice(k * BLOCK, (k + 1) * BLOCK)
            value = value - dot3((fh[:, there], fm[:, there]), (lh[here, there], lm[here, there]))
        value = dot3(split(value), (wh[j], wm[j]))
        hi, mid = split(value)
        fh[:, here] = hi
        fm[:, here] = mid
        out[:, here] = jnp.where(row >= lane + j * BLOCK, value, 0.0)


def solve_own(rows, factors, first_row):
    vmem = pl.BlockSpec(memory_space=pltpu.VMEM)
    return pl.pallas_call(
        solve_kernel,
        out_shape=jax.ShapeDtypeStruct(rows.shape, f32),
        in_specs=[pl.BlockSpec(memory_space=pltpu.SMEM)] + [vmem] * 5,
        out_specs=vmem,
        scratch_shapes=[pltpu.VMEM(rows.shape, bf16), pltpu.VMEM(rows.shape, bf16)],
        compiler_params=pltpu.CompilerParams(vmem_limit_bytes=40 << 20),
        cost_estimate=pl.CostEstimate(
            flops=10_000_000_000, bytes_accessed=20_000_000, transcendentals=0
        ),
        name="solve_own",
    )(first_row.reshape(1), rows, *factors)


def gram_of(left, right):
    return jnp.einsum("tr,tc->rc", left, right, preferred_element_type=f32)


def local(activations, expert_ids):
    tile_count = lax.axis_size("tile")
    group_count = lax.axis_size("expert")
    token_count, width = activations.shape
    capacity = 2 * token_count * expert_ids.shape[1] // group_count
    rows_device = width // tile_count
    tile_index = lax.axis_index("tile")
    first_row = tile_index * rows_device

    experts = jnp.arange(group_count, dtype=jnp.int32)
    routed = jnp.sum((expert_ids[..., None] == experts).astype(jnp.int32), axis=1)
    before = (
        jnp.arange(token_count)[:, None] > jnp.arange(token_count)[None, :]
    ).astype(bf16)
    slot = jnp.dot(before, routed.astype(bf16), preferred_element_type=f32).astype(jnp.int32)
    slots = jnp.arange(capacity, dtype=jnp.int32)
    selector = (routed[..., None] > 0) & (slot[..., None] == slots)
    selector = selector.reshape(token_count, group_count * capacity).astype(bf16)

    squares = jnp.sum(jnp.square(activations.astype(f32)), axis=1, keepdims=True)
    sq_hi, sq_rest = squares.astype(bf16), squares
    pieces = [jnp.ones((token_count, 1), bf16)]
    for _ in range(3):
        piece = sq_rest.astype(bf16)
        pieces.append(piece)
        sq_rest = sq_rest - piece.astype(f32)
    extra = jnp.concatenate(
        pieces + [jnp.zeros((token_count, EXTRA - len(pieces)), bf16)], axis=1
    )
    head = jnp.concatenate([activations[:, :LEAD], extra], axis=1)
    tail = activations[:, LEAD:]

    def dispatch(x):
        packed = lax.dot_general(
            selector, x, (((0,), (0,)), ((), ())), preferred_element_type=f32
        ).astype(bf16)
        packed = packed.reshape(group_count, capacity, x.shape[1])
        out = lax.all_to_all(packed, "expert", split_axis=0, concat_axis=0, tiled=True)
        return out.reshape(group_count * capacity, x.shape[1])

    got_head = dispatch(head)
    all_head = lax.all_gather(got_head, "tile", axis=0, tiled=True)
    got_tail = dispatch(tail)
    all_tail = lax.all_gather(got_tail, "tile", axis=0, tiled=True)

    sums = jnp.sum(all_head[:, LEAD : LEAD + 4].astype(f32), axis=0)
    scale = 2.0 / sums[0]
    damping = DAMP * ((sums[1] + (sums[2] + sums[3])) * scale) / width

    lead = all_head[:, :LEAD]
    gram = jnp.concatenate(
        [
            gram_of(lead, lead[:, :PANEL]),
            jnp.pad(gram_of(lead[:, PANEL:], lead[:, PANEL:]), ((PANEL, 0), (0, 0))),
        ],
        axis=1,
    )
    factors = cholesky_lead(gram, jnp.stack([scale, damping]))

    own = jnp.where(
        first_row < LEAD,
        lax.dynamic_slice_in_dim(lead, jnp.minimum(first_row, LEAD - rows_device), rows_device, 1),
        lax.dynamic_slice_in_dim(
            all_tail, jnp.maximum(first_row - LEAD, 0), rows_device, 1
        ),
    )
    rows = first_row + jnp.arange(rows_device, dtype=jnp.int32)
    hessian = []
    for part, start in ((lead, 0), (all_tail, LEAD)):
        columns = start + jnp.arange(part.shape[1], dtype=jnp.int32)
        hessian.append(
            gram_of(own, part) * scale
            + jnp.where(rows[:, None] == columns[None, :], damping, jnp.float32(0.0))
        )
    panels = solve_own(hessian[0], factors, first_row)
    return (jnp.concatenate(hessian, axis=1)[None], panels[None])


def solution(mesh):
    placed = (P(("expert", "tile"), None), P(("expert", "tile"), None))
    return jax.shard_map(
        local,
        mesh=mesh,
        in_specs=placed,
        out_specs=(P("expert", "tile", None), P("expert", "tile", None)),
        check_vma=False,
    )
```

time: 1120 us -> 338 us (0.30)
  other arithmetic: 390 us -> 17.8 us
  waiting for transfers between devices: 459 us -> 103 us
  Pallas kernels: 0 us -> 85.5 us
  matrix products: 98.9 us -> 53.4 us
  local copies, waits for them, and re-layouts: 56.5 us -> 16.2 us
  blocking collectives: 75.8 us -> 43.7 us
    another operation x51 -> x1, other arithmetic: 369 us -> 0.07 us  [local(): factors = cholesky_lead(gram, jnp.stack([scale, damping]))]
    psum x2 -> x0, waiting for transfers between devices: 289 us -> none  [panel_rows_fetch(): return lax.psum(placed, 'tile')]
    pallas_call x0 -> x2, Pallas kernels: none -> 85.5 us  [the longest x1 79.9 us: cholesky_lead(): pl.pallas_call(cholesky_kernel, out_shape=(jax.ShapeDtypeStruct((LEAD, LE...]
    all_gather x1 -> x2, waiting for transfers between devices: 163 us -> 103 us  [the longest x1 64.4 us: local(): all_head = lax.all_gather(got_head, 'tile', axis=0, tiled=True)]
    another operation x42 -> x0, matrix products: 46.9 us -> none  [the longest x22 27.3 us: local(): jax.scipy.linalg.solve_triangular(diagonal_factor, panel_block.T, lower=T...]
    unnamed x1 -> x0, blocking collectives: 39.8 us -> none
    another operation x52 -> x0, local copies, waits for them, and re-layouts: 35.7 us -> none  [the longest x39 35.3 us: local(): jax.scipy.linalg.solve_triangular(diagonal_factor, panel_block.T, lower=T...]
    all_to_all x1 -> x2, blocking collectives: 36 us -> 43.7 us  [dispatch(): lax.all_to_all(packed, 'expert', split_axis=0, concat_axis=0, tiled=True)]
  transfers between devices with their start and end apart: 4 -> 2, of which waited for: 4 -> 2; matrix products, arithmetic and copies ran while one was open for 2% -> 11% of each run, Pallas kernels for 0% -> 24%
where the time goes in v1:
time: 338 us; the launch traced here: 337 us
  waiting for transfers between devices  103 us (30%)
  Pallas kernels  85.5 us (25%)
  matrix products  53.4 us (16%)
  blocking collectives  43.7 us (13%)
  other arithmetic  17.8 us (5%)
  between operations  16.8 us (5%)
  local copies, waits for them, and re-layouts  16.2 us (5%)
    pallas_call x1, Pallas kernels, cholesky_lead(): pl.pallas_call(cholesky_kernel, out_shape=(jax.ShapeDtypeStruct((LEAD, LE...  79.9 us
    all_gather x1, waiting for transfers between devices, local(): all_head = lax.all_gather(got_head, 'tile', axis=0, tiled=True)  64.4 us
    dot_general x4, matrix products, gram_of(): return jnp.einsum('tr,tc->rc', left, right, preferred_element_type=f32)  51.4 us
    all_to_all x2, blocking collectives, dispatch(): lax.all_to_all(packed, 'expert', split_axis=0, concat_axis=0, tiled=True)  43.7 us
    all_gather x1, waiting for transfers between devices, local(): all_tail = lax.all_gather(got_tail, 'tile', axis=0, tiled=True)  39 us
    slice x1, local copies, waits for them, and re-layouts, local(): lead = all_head[:, :LEAD]  8.93 us
    broadcast_in_dim x1, other arithmetic, local(): return (jnp.concatenate(hessian, axis=1)[None], panels[None])  7.89 us
  transfers between devices with their start and end apart: 2, of which 2 were waited for; matrix products, arithmetic and copies ran while one was open for 11% of the time, Pallas kernels for 24%

profile of v1, /device:TPU:0, one launch (start us, length us, event | category | flops | bytes accessed | tf_op | source)
XLA Modules:
  0.0 337.0 jit_solution(15412308130257309665)
XLA Ops:
  7.2 1.3 multiply_reduce_fusion
  8.5 0.9 slice.33
  9.4 0.7 convert_reduce_fusion.1
  11.2 16.6 %all_to_all.10 = bf16[8,24,1664]{2,1,0:T(8,128)(2,1)} all-to-all(bf16[8,24,1664]{2,1,0:T(8,128)(2,1)S(1)} %bitcast.40), channel_id=1, replica_groups=mesh['expert'=8,'tile'=16] {'expert'}, dimensions={0} | all-to-all | bytes 1277952 | tf_op jit(solution)/shard_map/all_to_all | solution.py:257
  28.0 1.6 convolution_convert_fusion
  29.6 27.0 %all_to_all.11 = bf16[8,24,4608]{2,1,0:T(8,128)(2,1)} all-to-all(bf16[8,24,4608]{2,1,0:T(8,128)(2,1)S(1)} %bitcast.38), channel_id=1, replica_groups=mesh['expert'=8,'tile'=16] {'expert'}, dimensions={0} | all-to-all | bytes 3538944 | tf_op jit(solution)/shard_map/all_to_all | solution.py:257
  56.6 0.6 iota_add_fusion.1
  57.2 0.6 iota_add_fusion
  57.8 64.4 %all-gather.3.cloned.1.call-done = bf16[3072,1664]{1,0:T(8,128)(2,1)} async-done(((bf16[192,1664]{1,0:T(8,128)(2,1)}), bf16[3072,1664]{1,0:T(8,128)(2,1)}) %all-gather.3.cloned.1.call-update) | async-done | bytes 10223632 | tf_op jit(solution)/shard_map/all_gather | solution.py:261
  122.2 1.6 convert_reduce_fusion
  123.8 0.7 fusion.13
  127.1 8.9 %slice.43 = bf16[3072,1536]{1,0:T(8,128)(2,1)} slice(bf16[3072,1664]{1,0:T(8,128)(2,1)} %all-gather.3.cloned.1.call-done), slice={[0:3072], [0:1536]} | slice | bytes 18874368 | tf_op jit(solution)/shard_map/slice | solution.py:269
  136.1 7.2 %fusion.1 = f32[768,768]{1,0:T(8,128)S(1)} fusion(bf16[3072,1664]{1,0:T(8,128)(2,1)} %all-gather.3.cloned.1.call-done), kind=kOutput, calls=%fused_computation.6 | convolution fusion | flops 3623878656 | bytes 7077888 | tf_op jit(solution)/shard_map/tr,tc->rc/dot_general | solution.py:217
  143.3 11.7 %fusion.3 = f32[1536,768]{1,0:T(8,128)S(1)} fusion(bf16[3072,1664]{1,0:T(8,128)(2,1)} %all-gather.3.cloned.1.call-done), kind=kOutput, calls=%fused_computation.8 | convolution fusion | flops 7247757312 | bytes 18874368 | tf_op jit(solution)/shard_map/tr,tc->rc/dot_general | solution.py:217
  155.0 5.0 %select_maximum_fusion.gram = f32[1536,1536]{1,0:T(8,128)} fusion(f32[768,768]{1,0:T(8,128)S(1)} %fusion.1, f32[1536,768]{1,0:T(8,128)S(1)} %fusion.3), kind=kLoop, calls=%fused_computation | loop fusion | flops 7077888 | bytes 16515072 | tf_op jit(solution)/shard_map/concatenate | solution.py:270
  159.9 79.9 %cholesky_lead.1 = (bf16[1536,1536]{1,0:T(8,128)(2,1)S(1)}, bf16[1536,1536]{1,0:T(8,128)(2,1)S(1)}, bf16[6,256,256]{2,1,0:T(8,128)(2,1)S(1)}, bf16[6,256,256]{2,1,0:T(8,128)(2,1)S(1)}) custom-call(f32[2]{0:T(128)S(1)} %pad_maximum_fusion.scalars, f32[1536,1536]{1,0:T(8,128)} %select_maximum_fusion.gram), custom_call_target="tpu_custom_call" | custom-call | flops 149999992832 | bytes 30000000 | tf_op jit(solution)/shard_map/cholesky_lead/pallas_call | solution.py:158
  239.9 2.1 copy-done
  242.0 2.1 copy-done.1
  244.2 0.9 copy-done.3
  245.0 39.0 %all-gather.5.cloned.1.call-done = bf16[3072,4608]{1,0:T(8,128)(2,1)} async-done(((bf16[192,4608]{1,0:T(8,128)(2,1)}), bf16[3072,4608]{1,0:T(8,128)(2,1)}) %all-gather.5.cloned.1.call-update) | async-done | bytes 28311568 | tf_op jit(solution)/shard_map/all_gather | solution.py:263
  284.0 11.3 %fusion.5.rows = f32[384,1536]{1,0:T(8,128)S(1)} fusion(bf16[3072,1536]{1,0:T(8,128)(2,1)} %slice.43, f32[]{:T(128)} %div.11, s32[384]{0:T(512)S(1)} %copy-done.6, f32[]{:T(128)} %bitcast.7, bf16[3072,4608]{1,0:T(8,128)(2,1)} %all-gather.5.cloned.1.call-done, s32[]{:T(128)S(6)} %max.3, s32[]{:T(128)S(6)} %select_n.21, pred[]{:T(512)S(6)} %lt.7), kind=kOutput, calls=%fused_computation.11 | convolution fusion | flops 3627417600 | bytes 16517641 | tf_op jit(solution)/shard_map/tr,tc->rc/dot_general | solution.py:217
  295.3 21.2 %fusion = f32[384,4608]{1,0:T(8,128)} fusion(bf16[3072,4608]{1,0:T(8,128)(2,1)} %all-gather.5.cloned.1.call-done, f32[]{:T(128)} %div.11, s32[4608]{0:T(1024)S(1)} %copy-done.5, f32[]{:T(128)} %bitcast.7, s32[384]{0:T(512)S(1)} %copy-done.6, s32[]{:T(128)S(6)} %max.3, bf16[3072,1536]{1,0:T(8,128)(2,1)} %slice.43, s32[]{:T(128)S(6)} %select_n.21, pred[]{:T(512)S(6)} %lt.7), kind=kOutput, calls=%fused_computation.4 | convolution fusion | flops 10879893504 | bytes 40129032 | tf_op jit(solution)/shard_map/tr,tc->rc/dot_general | solution.py:217
  316.6 7.9 %maximum_bitcast_fusion = f32[1,384,6144]{2,1,0:T(8,128)} fusion(f32[384,4608]{1,0:T(8,128)} %fusion, f32[384,1536]{1,0:T(8,128)S(1)} %fusion.5.rows), kind=kLoop, calls=%fused_computation.2 | loop fusion | flops 2359296 | bytes 18874368 | tf_op jit(solution)/shard_map/broadcast_in_dim | solution.py:295
  324.5 5.6 %solve_own.1 = f32[384,1536]{1,0:T(8,128)} custom-call(s32[1]{0:T(128)} %bitcast.10.first_row, f32[384,1536]{1,0:T(8,128)S(1)} %fusion.5.rows, bf16[1536,1536]{1,0:T(8,128)(2,1)S(1)} %bitcast.36, bf16[1536,1536]{1,0:T(8,128)(2,1)S(1)} %copy-done.2, bf16[6,256,256]{2,1,0:T(8,128)(2,1)S(1)} %get-tuple-element.8.wh, bf16[6,256,256]{2,1,0:T(8,128)(2,1)S(1)} %copy-done.4), custom_call_target="tpu_custom_call" | custom-call | flops 10000000000 | bytes 20000000 | tf_op jit(solution)/shard_map/solve_own/pallas_call | solution.py:202
  (35 shorter events, 1.3 us)
Async XLA Ops:
  7.2 115.1 %all-gather.3.cloned.1.call-start = ((), (), s32[]{:S(2)}) async-start(), calls=%async_computation.2 | async-start | bytes 10862592 | tf_op jit(solution)/shard_map/all_gather | solution.py:261
  27.9 256.1 %all-gather.5.cloned.1.call-start = ((), (), s32[]{:S(2)}) async-start(), calls=%async_computation.3 | async-start | bytes 30081024 | tf_op jit(solution)/shard_map/all_gather | solution.py:263
  159.9 124.1 %copy-start.6 = (s32[384]{0:T(512)S(1)}, s32[384]{0:T(512)}, u32[]{:S(2)}) copy-start(s32[384]{0:T(512)} %iota_add_fusion.1) | copy-start | bytes 4612
  239.9 2.1 copy-start
  242.0 2.1 copy-start.1
  244.2 0.9 copy-start.3
  245.0 50.3 %copy-start.5 = (s32[4608]{0:T(1024)S(1)}, s32[4608]{0:T(1024)}, u32[]{:S(2)}) copy-start(s32[4608]{0:T(1024)} %iota_add_fusion) | copy-start | bytes 55300
  284.0 40.4 %slice-start = ((s8[4718592]{0:T(1024)(128)(4,1)}), s8[4194304]{0:T(1024)(128)(4,1)S(1)}, s32[]{:S(2)}) async-start(s8[4718592]{0:T(1024)(128)(4,1)} %bitcast.35), calls=%async_computation.4 | async-start | bytes 8388608
  295.3 29.2 %slice-start.1 = ((s8[4718592]{0:T(1024)(128)(4,1)}), s8[524288]{0:T(1024)(128)(4,1)S(1)}, s32[]{:S(2)}) async-start(s8[4718592]{0:T(1024)(128)(4,1)} %bitcast.35), calls=%async_computation.5 | async-start | bytes 1048576
  316.6 7.9 %copy-start.2 = (bf16[1536,1536]{1,0:T(8,128)(2,1)S(1)}, bf16[1536,1536]{1,0:T(8,128)(2,1)}, u32[]{:S(2)}) copy-start(bf16[1536,1536]{1,0:T(8,128)(2,1)} %copy-done.1) | copy-start | bytes 14155780
  316.6 7.9 %copy-start.4 = (bf16[6,256,256]{2,1,0:T(8,128)(2,1)S(1)}, bf16[6,256,256]{2,1,0:T(8,128)(2,1)}, u32[]{:S(2)}) copy-start(bf16[6,256,256]{2,1,0:T(8,128)(2,1)} %copy-done.3) | copy-start | bytes 2359300
Sparse Core Ops, SparseCore 0:
  28.0 94.1 all-gather.2
  124.7 159.3 all-gather.4
